TPU v7x, 256 devices: a whole 4x4x8 slice. The times are simulated.
256 devices in a mesh: tm: 32 (over y, z), eval: 8 (over x, core).
Axes of the slice: x: 4, y: 4, z: 8, core: 2. Of those that a mesh axis runs over, the one named last changes fastest.
Arguments:
- hidden: bfloat16 [512, 1024, 1536], P('tm', 'eval'), may hold values from -9 to 9
- modulation: float32 [512, 2, 1536], P('tm'), may hold values from -2 to 3
- head_weight: bfloat16 [64, 1536], replicated, may hold values from -1 to 1
- real_score: bfloat16 [64, 21, 16, 4096], P('eval', None, None, 'tm'), may hold values from -152917 to 152917
- fake_score: bfloat16 [64, 21, 16, 4096], P('eval', None, None, 'tm'), may hold values from -152917 to 152917
- window_start: int32 [64], P('eval'), may hold values from 0 to 491, as said below
- timestep: int32 [64], P('eval'), may hold values from 20 to 999
Outputs:
- d_hidden: bfloat16 [512, 1024, 1536], P('tm', 'eval')
- head_grad: float32 [64, 1536], replicated
- mod_grad: float32 [512, 2, 1536], P('tm')
Inputs may be any that keep to these rules, and one draw needn't show every extreme that they name: `window_start`: every window lies inside the rollout; one window starts at frame 0 and one at the last possible frame.
All inputs are finite; a program needn't handle non-finite values.
Results may differ from a plain program's by a relative error of at most 0.0012.
The roundings to bfloat16 on the way count: a program that leaves them out, or rounds other values in their place, can miss the bound.
Values may be sent and summed in bfloat16 or wider, within the bound.
No kernel may reach another device: no remote copies, remote signals or barrier semaphores. Data moves between devices by JAX's collectives and lax.ppermute only.
A program may use at most 128 MiB of HBM per device.

v0:
```python
import jax
import jax.numpy as jnp
from jax import lax
from jax.sharding import PartitionSpec as P

C = 16
PATCH = 4
WIN = 21
TOK = 1024


def layer_norm(values_in):
    values = values_in.astype(jnp.float32)
    center = jnp.mean(values, axis=-1, keepdims=True)
    shifted = values - center
    inv_std = lax.rsqrt(jnp.mean(shifted * shifted, axis=-1, keepdims=True) + 1e-06)
    return (shifted * inv_std, inv_std)


def per_device(hidden, modulation, head_weight, real_score, fake_score, window_start, timestep):
    frames_dev, tok_dev, width = hidden.shape
    shift = modulation[:, 0][:, None, :]
    scale = modulation[:, 1][:, None, :]
    normed, inv_std = layer_norm(hidden)
    adapted = (normed * (1.0 + scale) + shift).astype(jnp.bfloat16)
    head_out = jnp.einsum("ftd,od->fto", adapted, head_weight, preferred_element_type=jnp.float32)
    latent = head_out.astype(jnp.bfloat16).reshape(frames_dev, tok_dev, C, PATCH)
    latent = latent.transpose(0, 2, 1, 3).reshape(frames_dev, C, tok_dev * PATCH)
    frame_whole = lax.all_gather(latent, "eval", axis=2, tiled=True)
    latent_all = lax.all_to_all(frame_whole, "tm", split_axis=2, concat_axis=0, tiled=True)
    pixel_block = latent_all.shape[2]
    frame_index = window_start[:, None] + jnp.arange(WIN, dtype=jnp.int32)[None, :]
    window_latent = latent_all[frame_index].astype(jnp.float32)
    real_values = real_score.astype(jnp.float32)
    fake_values = fake_score.astype(jnp.float32)
    abs_sums = jnp.sum(jnp.abs(window_latent - real_values), axis=(1, 2, 3))
    totals = lax.psum(abs_sums, "tm")
    normalizer = totals / (WIN * C * PATCH * TOK) + 1e-05
    weight = timestep.astype(jnp.float32) / 1000.0 / normalizer
    window_grad = weight[:, None, None, None] * (fake_values - real_values)
    group_grad = (
        jnp.zeros(latent_all.shape, jnp.float32)
        .at[frame_index.reshape(-1)]
        .add(window_grad.reshape(-1, C, pixel_block))
    )
    home = lax.all_to_all(group_grad, "tm", split_axis=0, concat_axis=2, tiled=True)
    owner_grad = lax.psum_scatter(home, "eval", scatter_dimension=2, tiled=True)
    upstream = owner_grad.reshape(frames_dev, C, tok_dev, PATCH).transpose(0, 2, 1, 3)
    upstream = upstream.reshape(frames_dev, tok_dev, C * PATCH).astype(jnp.bfloat16)
    d_adapted = jnp.einsum("fto,od->ftd", upstream, head_weight, preferred_element_type=jnp.float32)
    head_part = jnp.einsum("fto,ftd->od", upstream, adapted, preferred_element_type=jnp.float32)
    mod_part = jnp.stack([jnp.sum(d_adapted, axis=1), jnp.sum(d_adapted * normed, axis=1)], axis=1)
    head_grad = lax.psum(head_part, ("tm", "eval"))
    mod_grad = lax.psum(mod_part, "eval")
    d_normed = d_adapted * (1.0 + scale)
    d_hidden = inv_std * (
        d_normed
        - jnp.mean(d_normed, axis=-1, keepdims=True)
        - normed * jnp.mean(d_normed * normed, axis=-1, keepdims=True)
    )
    return (d_hidden.astype(jnp.bfloat16), head_grad, mod_grad)


def solution(mesh):
    placed = (
        P("tm", "eval", None),
        P("tm", None, None),
        P(),
        P("eval", None, None, "tm"),
        P("eval", None, None, "tm"),
        P("eval"),
        P("eval"),
    )
    return jax.shard_map(
        per_device,
        mesh=mesh,
        in_specs=placed,
        out_specs=(P("tm", "eval", None), P(), P("tm", None, None)),
        check_vma=False,
    )
```

profile of v0, /device:TPU:1, one launch (start us, length us, event | category | flops | bytes accessed | tf_op | source)
XLA Modules:
  0.0 757.5 jit_solution(7772980234880290092)
XLA Ops:
  7.2 3.8 convert_reduce_fusion
  11.1 4.6 fusion.13
  15.9 3.1 fusion.24
  19.0 3.2 copy.49
  22.2 2.3 copy.50
  24.5 32.2 %all-gather.2.cloned.1.call-done = bf16[16,16,4096]{2,1,0:T(8,128)(2,1)} async-done(((bf16[16,16,512]{2,1,0:T(8,128)(2,1)}), bf16[16,16,4096]{2,1,0:T(8,128)(2,1)}) %all-gather.2.cloned.1.call-update) | async-done | bytes 2097168 | tf_op jit(solution)/shard_map/all_gather | solution.py:29
  56.7 15.4 %copy.51 = bf16[16,16,4096]{1,0,2:T(8,128)(2,1)} copy(bf16[16,16,4096]{2,1,0:T(8,128)(2,1)} %all-gather.2.cloned.1.call-done) | data formatting | bytes 4194304 | tf_op jit(solution)/shard_map/all_gather | solution.py:29
  72.0 20.8 %reshape.132 = bf16[32,2,16384]{2,1,0:T(2,128)(2,1)} reshape(bf16[4096,16,16]{2,1,0:T(8,128)(2,1)} %bitcast.43) | data formatting | bytes 4194304
  92.8 9.6 %all-to-all-start = ((bf16[32,2,16384]{2,1,0:T(2,128)(2,1)}), bf16[32,2,16384]{2,1,0:T(2,128)(2,1)S(1)}, u32[]{:S(2)}, u32[]{:S(2)}) async-start(bf16[32,2,16384]{2,1,0:T(2,128)(2,1)} %reshape.132), calls=%async_computation | async-start | bytes 4194304 | tf_op jit(solution)/shard_map/all_to_all | solution.py:30
  102.8 48.5 %all-to-all-done = bf16[32,2,16384]{2,1,0:T(2,128)(2,1)S(1)} async-done(((bf16[32,2,16384]{2,1,0:T(2,128)(2,1)}), bf16[32,2,16384]{2,1,0:T(2,128)(2,1)S(1)}, u32[]{:S(2)}, u32[]{:S(2)}) %all-to-all-start) | async-done | bytes 2097184 | tf_op jit(solution)/shard_map/all_to_all | solution.py:30
  151.3 14.4 %reshape.133 = bf16[4096,16,16]{2,1,0:T(8,128)(2,1)} reshape(bf16[32,2,16384]{2,1,0:T(2,128)(2,1)S(1)} %all-to-all-done) | data formatting | bytes 4194304
  165.7 14.4 %copy.53 = bf16[32,16,16,128]{3,2,1,0:T(8,128)(2,1)S(1)} copy(bf16[32,16,16,128]{2,1,3,0:T(8,128)(2,1)} %bitcast.44) | data formatting | bytes 4194304 | tf_op jit(solution)/shard_map/all_to_all | solution.py:30
  180.1 1.6 gather_fusion
  181.7 1.4 fusion.22
  183.1 60.2 %psum.21 = f32[8]{0:T(128)S(1)} all-reduce(f32[8]{0:T(128)S(1)} %fusion.22), channel_id=1, replica_groups=mesh['tm'=32,'eval'=8] {'tm'}, use_global_device_ids=true, to_apply=%region_3.0 | all-reduce | flops 8 | bytes 64 | tf_op jit(solution)/shard_map/psum | solution.py:37
  243.4 1.3 fusion.23
  244.7 2.3 broadcast_in_dim.2
  247.0 19.7 %scatter_fusion = f32[512,16,128]{2,1,0:T(8,128)} fusion(f32[512,16,128]{2,1,0:T(8,128)} %broadcast_in_dim.2, s32[168]{0:T(256)S(1)} %bitcast.59, f32[168,16,128]{2,1,0:T(8,128)S(1)} %bitcast.51), kind=kCustom, calls=%fused_computation.1 | custom fusion | flops 344064 | bytes 4129440 | tf_op jit(solution)/shard_map/scatter-add | solution.py:44
  266.7 83.4 %all_to_all.36 = f32[512,16,128]{2,1,0:T(8,128)S(1)} all-to-all(f32[512,16,128]{2,1,0:T(8,128)} %scatter_fusion), channel_id=1, replica_groups=mesh['tm'=32,'eval'=8] {'tm'}, dimensions={0} | all-to-all | bytes 8388608 | tf_op jit(solution)/shard_map/all_to_all | solution.py:46
  350.1 2.5 copy.76
  352.7 50.7 %reduce-scatter.2.cloned.1.call-done = f32[16,16,512]{2,1,0:T(8,128)} async-done(((f32[16,16,4096]{2,1,0:T(8,128)}), f32[16,16,512]{2,1,0:T(8,128)}) %reduce-scatter.2.cloned.1.call-update) | async-done | bytes 524304 | tf_op jit(solution)/shard_map/reduce_scatter | solution.py:47
  403.4 1.1 convert_element_type.43
  404.5 2.8 copy.55
  407.3 4.0 copy.56
  411.3 10.1 %fusion.12 = (f32[16,1536]{1,0:T(8,128)S(1)}, f32[16,128]{1,0:T(8,128)S(1)}, f32[16,128]{1,0:T(8,128)S(1)}, f32[16,1536]{1,0:T(8,128)S(1)}, f32[16,128,1536]{2,1,0:T(8,128)}) fusion(bf16[16,128,1536]{2,1,0:T(8,128)(2,1)} %param.7, f32[16,128]{1,0:T(8,128)S(1)} %add_rsqrt_fusion, f32[16,128]{1,0:T(8,128)S(1)} %broadcast_multiply_fusion.2, ...), kind=kOutput, calls=%fused_computation.16 | convolution fusion | flops 434057216 | bytes 19660800 | tf_op jit(solution)/shard_map/fto,od->ftd/dot_general | solution.py:50
  421.4 3.5 fusion.18
  424.9 0.7 pad_maximum_fusion
  426.2 10.5 %fusion.11 = bf16[16,128,1536]{2,1,0:T(8,128)(2,1)} fusion(bf16[16,128,1536]{2,1,0:T(8,128)(2,1)} %param.7, f32[16,128,1536]{2,1,0:T(8,128)} %get-tuple-element.24, f32[16,128]{1,0:T(8,128)S(1)} %broadcast_multiply_fusion, f32[16,128]{1,0:T(8,128)S(1)} %broadcast_multiply_fusion.1, f32[16,1536]{1,0:T(8,128)S(1)} %get-tuple-element.26, ...), kind=kLoop, calls=%fused_computation.15 | loop fusion | flops 28311552 | bytes 25296896 | tf_op jit(solution)/shard_map/convert_element_type | solution.py:61
  436.7 53.9 %all-reduce.5.cloned.1.call-done = f32[16,2,1536]{2,0,1:T(8,128)} async-done(((f32[16,2,1536]{2,0,1:T(8,128)}), f32[16,2,1536]{2,0,1:T(8,128)}) %all-reduce.5.cloned.1.call-update) | async-done | bytes 196624 | tf_op jit(solution)/shard_map/psum | solution.py:54
  490.5 1.8 copy.59
  492.3 256.9 %all-reduce.3.cloned.1.call-done = f32[64,1536]{1,0:T(8,128)} async-done(((f32[64,1536]{1,0:T(8,128)}), f32[64,1536]{1,0:T(8,128)}) %all-reduce.3.cloned.1.call-update) | async-done | bytes 393232 | tf_op jit(solution)/shard_map/psum | solution.py:53
  749.2 1.8 copy.80
  (38 shorter events, 1.3 us)
Async XLA Ops:
  7.2 8.7 %copy-start = (bf16[64,1536]{1,0:T(8,128)(2,1)S(1)}, bf16[64,1536]{1,0:T(8,128)(2,1)}, u32[]{:S(2)}) copy-start(bf16[64,1536]{1,0:T(8,128)(2,1)} %param.9) | copy-start | bytes 589828
  7.2 8.5 %copy-start.3 = (f32[16,2,1536]{2,1,0:T(2,128)S(1)}, f32[16,2,1536]{2,1,0:T(2,128)}, u32[]{:S(2)}) copy-start(f32[16,2,1536]{2,1,0:T(2,128)} %param.8) | copy-start | bytes 589828
  7.2 49.5 %all-gather.2.cloned.1.call-start = ((), (), s32[]{:S(2)}) async-start(), calls=%async_computation.3 | async-start | bytes 2359296 | tf_op jit(solution)/shard_map/all_gather | solution.py:29
  7.2 8.7 %copy-start.1 = (bf16[16,128,1536]{2,1,0:T(8,128)(2,1)S(1)}, bf16[16,128,1536]{2,1,0:T(8,128)(2,1)}, u32[]{:S(2)}) copy-start(bf16[16,128,1536]{2,1,0:T(8,128)(2,1)} %param.7) | copy-start | bytes 18874372
  72.0 30.4 %copy-start.4 = (s32[8]{0:T(128)S(1)}, s32[8]{0:T(128)}, u32[]{:S(2)}) copy-start(s32[8]{0:T(128)} %param.12) | copy-start | bytes 100
  92.8 58.5 %all-to-all-start = ((bf16[32,2,16384]{2,1,0:T(2,128)(2,1)}), bf16[32,2,16384]{2,1,0:T(2,128)(2,1)S(1)}, u32[]{:S(2)}, u32[]{:S(2)}) async-start(bf16[32,2,16384]{2,1,0:T(2,128)(2,1)} %reshape.132), calls=%async_computation | async-start | bytes 4194304 | tf_op jit(solution)/shard_map/all_to_all | solution.py:30
  102.4 301.0 %reduce-scatter.2.cloned.1.call-start = ((), (), s32[]{:S(2)}) async-start(), calls=%async_computation.4 | async-start | bytes 4718592 | tf_op jit(solution)/shard_map/reduce_scatter | solution.py:47
  165.7 16.0 %copy-start.2 = (bf16[8,21,16,128]{3,2,1,0:T(8,128)(2,1)S(1)}, bf16[8,21,16,128]{3,2,1,0:T(8,128)(2,1)}, u32[]{:S(2)}) copy-start(bf16[8,21,16,128]{3,2,1,0:T(8,128)(2,1)} %param.10) | copy-start | bytes 2064388
  165.7 77.7 %copy-start.5 = (s32[8]{0:T(128)S(1)}, s32[8]{0:T(128)}, u32[]{:S(2)}) copy-start(s32[8]{0:T(128)} %param.13) | copy-start | bytes 100
  352.7 137.9 %all-reduce.5.cloned.1.call-start = ((), (), s32[]{:S(2)}) async-start(), calls=%async_computation.6 | async-start | bytes 393216 | tf_op jit(solution)/shard_map/psum | solution.py:54
  407.3 14.2 %slice-start = ((s8[6291456]{0:T(1024)(128)(4,1)}), s8[2097152]{0:T(1024)(128)(4,1)S(1)}, s32[]{:S(2)}) async-start(s8[6291456]{0:T(1024)(128)(4,1)} %bitcast.45), calls=%async_computation.7 | async-start | bytes 4194304
  411.3 10.1 %slice-start.1 = ((s8[6291456]{0:T(1024)(128)(4,1)}), s8[4194304]{0:T(1024)(128)(4,1)S(1)}, s32[]{:S(2)}) async-start(s8[6291456]{0:T(1024)(128)(4,1)} %bitcast.45), calls=%async_computation.8 | async-start | bytes 8388608
  425.6 323.6 %all-reduce.3.cloned.1.call-start = ((), (), s32[]{:S(2)}) async-start(), calls=%async_computation.5 | async-start | bytes 786432 | tf_op jit(solution)/shard_map/psum | solution.py:53
Sparse Core Ops, SparseCore 0:
  24.6 31.9 all-gather.1
  352.8 50.5 reduce-scatter.1
  425.7 64.7 all-reduce.4
  496.5 252.6 all-reduce.2
where the time goes:
time: 760 us; the launch traced here: 758 us
  waiting for transfers between devices  443 us (58%)
  blocking collectives  144 us (19%)
  local copies, waits for them, and re-layouts  87.5 us (12%)
  other arithmetic  43.3 us (6%)
  matrix products  16.6 us (2%)
  between operations  14 us (2%)
  starting transfers between devices  9.73 us (1%)
    psum x1, waiting for transfers between devices, per_device(): head_grad = lax.psum(head_part, ('tm', 'eval'))  257 us
    all_to_all x1, blocking collectives, per_device(): lax.all_to_all(group_grad, 'tm', split_axis=0, concat_axis=2, tiled=True)  83.4 us
    psum x1, blocking collectives, per_device(): totals = lax.psum(abs_sums, 'tm')  60.2 us
    psum x1, waiting for transfers between devices, per_device(): mod_grad = lax.psum(mod_part, 'eval')  53.9 us
    reduce_scatter x1, waiting for transfers between devices, per_device(): owner_grad = lax.psum_scatter(home, 'eval', scatter_dimension=2, tiled=True)  50.7 us
    all_to_all x1, waiting for transfers between devices, per_device(): lax.all_to_all(frame_whole, 'tm', split_axis=2, concat_axis=0, tiled=True)  48.5 us
    unnamed x20, local copies, waits for them, and re-layouts  38.7 us
    all_gather x1, waiting for transfers between devices, per_device(): frame_whole = lax.all_gather(latent, 'eval', axis=2, tiled=True)  32.2 us
  transfers between devices with their start and end apart: 5, of which 5 were waited for; matrix products, arithmetic and copies ran while one was open for 2% of the time, Pallas kernels for 0%

commit v1 on v0

--- a/solution.py
+++ b/solution.py
@@ -50,7 +50,8 @@
     d_adapted = jnp.einsum("fto,od->ftd", upstream, head_weight, preferred_element_type=jnp.float32)
     head_part = jnp.einsum("fto,ftd->od", upstream, adapted, preferred_element_type=jnp.float32)
     mod_part = jnp.stack([jnp.sum(d_adapted, axis=1), jnp.sum(d_adapted * normed, axis=1)], axis=1)
-    head_grad = lax.psum(head_part, ("tm", "eval"))
+    half = lax.psum(head_part, "eval")
+    head_grad = lax.psum(half, "tm")
     mod_grad = lax.psum(mod_part, "eval")
     d_normed = d_adapted * (1.0 + scale)
     d_hidden = inv_std * (

time: 760 us -> 653 us (0.86)
  waiting for transfers between devices: 443 us -> 333 us
    psum x2, waiting for transfers between devices: 311 us -> 202 us  [the longest x1 136 us: per_device(): head_grad = lax.psum(half, 'tm')]
    unnamed x20 -> x22, local copies, waits for them, and re-layouts: 38.7 us -> 37.8 us
where the time goes in v1:
time: 653 us; the launch traced here: 647 us
  waiting for transfers between devices  333 us (51%)
  blocking collectives  144 us (22%)
  local copies, waits for them, and re-layouts  86.6 us (13%)
  other arithmetic  43.3 us (7%)
  matrix products  16.6 us (3%)
  between operations  14 us (2%)
  starting transfers between devices  9.73 us (1%)
    psum x1, waiting for transfers between devices, per_device(): head_grad = lax.psum(half, 'tm')  136 us
    all_to_all x1, blocking collectives, per_device(): lax.all_to_all(group_grad, 'tm', split_axis=0, concat_axis=2, tiled=True)  83.4 us
    psum x1, waiting for transfers between devices, per_device(): half = lax.psum(head_part, 'eval')  66.1 us
    psum x1, blocking collectives, per_device(): totals = lax.psum(abs_sums, 'tm')  60.2 us
    reduce_scatter x1, waiting for transfers between devices, per_device(): owner_grad = lax.psum_scatter(home, 'eval', scatter_dimension=2, tiled=True)  50.7 us
    all_to_all x1, waiting for transfers between devices, per_device(): lax.all_to_all(frame_whole, 'tm', split_axis=2, concat_axis=0, tiled=True)  48.5 us
    unnamed x22, local copies, waits for them, and re-layouts  37.8 us
    all_gather x1, waiting for transfers between devices, per_device(): frame_whole = lax.all_gather(latent, 'eval', axis=2, tiled=True)  32.2 us
  transfers between devices with their start and end apart: 5, of which 5 were waited for; matrix products, arithmetic and copies ran while one was open for 2% of the time, Pallas kernels for 0%

profile of v1, /device:TPU:1, one launch (start us, length us, event | category | flops | bytes accessed | tf_op | source)
XLA Modules:
  0.0 647.1 jit_solution(4845662212469694354)
XLA Ops:
  7.2 3.8 convert_reduce_fusion
  11.1 4.6 fusion.13
  15.9 3.1 fusion.24
  19.0 3.2 copy.49
  22.2 2.3 copy.50
  24.5 32.2 %all-gather.2.cloned.1.call-done = bf16[16,16,4096]{2,1,0:T(8,128)(2,1)} async-done(((bf16[16,16,512]{2,1,0:T(8,128)(2,1)}), bf16[16,16,4096]{2,1,0:T(8,128)(2,1)}) %all-gather.2.cloned.1.call-update) | async-done | bytes 2097168 | tf_op jit(solution)/shard_map/all_gather | solution.py:29
  56.7 15.4 %copy.51 = bf16[16,16,4096]{1,0,2:T(8,128)(2,1)} copy(bf16[16,16,4096]{2,1,0:T(8,128)(2,1)} %all-gather.2.cloned.1.call-done) | data formatting | bytes 4194304 | tf_op jit(solution)/shard_map/all_gather | solution.py:29
  72.0 20.8 %reshape.132 = bf16[32,2,16384]{2,1,0:T(2,128)(2,1)} reshape(bf16[4096,16,16]{2,1,0:T(8,128)(2,1)} %bitcast.43) | data formatting | bytes 4194304
  92.8 9.6 %all-to-all-start = ((bf16[32,2,16384]{2,1,0:T(2,128)(2,1)}), bf16[32,2,16384]{2,1,0:T(2,128)(2,1)S(1)}, u32[]{:S(2)}, u32[]{:S(2)}) async-start(bf16[32,2,16384]{2,1,0:T(2,128)(2,1)} %reshape.132), calls=%async_computation | async-start | bytes 4194304 | tf_op jit(solution)/shard_map/all_to_all | solution.py:30
  102.8 48.5 %all-to-all-done = bf16[32,2,16384]{2,1,0:T(2,128)(2,1)S(1)} async-done(((bf16[32,2,16384]{2,1,0:T(2,128)(2,1)}), bf16[32,2,16384]{2,1,0:T(2,128)(2,1)S(1)}, u32[]{:S(2)}, u32[]{:S(2)}) %all-to-all-start) | async-done | bytes 2097184 | tf_op jit(solution)/shard_map/all_to_all | solution.py:30
  151.3 14.4 %reshape.133 = bf16[4096,16,16]{2,1,0:T(8,128)(2,1)} reshape(bf16[32,2,16384]{2,1,0:T(2,128)(2,1)S(1)} %all-to-all-done) | data formatting | bytes 4194304
  165.7 14.4 %copy.53 = bf16[32,16,16,128]{3,2,1,0:T(8,128)(2,1)S(1)} copy(bf16[32,16,16,128]{2,1,3,0:T(8,128)(2,1)} %bitcast.44) | data formatting | bytes 4194304 | tf_op jit(solution)/shard_map/all_to_all | solution.py:30
  180.1 1.6 gather_fusion
  181.7 1.4 fusion.22
  183.1 60.2 %psum.28 = f32[8]{0:T(128)S(1)} all-reduce(f32[8]{0:T(128)S(1)} %fusion.22), channel_id=1, replica_groups=mesh['tm'=32,'eval'=8] {'tm'}, use_global_device_ids=true, to_apply=%region_3.0 | all-reduce | flops 8 | bytes 64 | tf_op jit(solution)/shard_map/psum | solution.py:37
  243.4 1.3 fusion.23
  244.7 2.3 broadcast_in_dim.2
  247.0 19.7 %scatter_fusion = f32[512,16,128]{2,1,0:T(8,128)} fusion(f32[512,16,128]{2,1,0:T(8,128)} %broadcast_in_dim.2, s32[168]{0:T(256)S(1)} %bitcast.59, f32[168,16,128]{2,1,0:T(8,128)S(1)} %bitcast.51), kind=kCustom, calls=%fused_computation.1 | custom fusion | flops 344064 | bytes 4129440 | tf_op jit(solution)/shard_map/scatter-add | solution.py:44
  266.7 83.4 %all_to_all.36 = f32[512,16,128]{2,1,0:T(8,128)S(1)} all-to-all(f32[512,16,128]{2,1,0:T(8,128)} %scatter_fusion), channel_id=1, replica_groups=mesh['tm'=32,'eval'=8] {'tm'}, dimensions={0} | all-to-all | bytes 8388608 | tf_op jit(solution)/shard_map/all_to_all | solution.py:46
  350.1 2.5 copy.76
  352.7 50.7 %reduce-scatter.2.cloned.1.call-done = f32[16,16,512]{2,1,0:T(8,128)} async-done(((f32[16,16,4096]{2,1,0:T(8,128)}), f32[16,16,512]{2,1,0:T(8,128)}) %reduce-scatter.2.cloned.1.call-update) | async-done | bytes 524304 | tf_op jit(solution)/shard_map/reduce_scatter | solution.py:47
  403.4 1.1 convert_element_type.43
  404.5 2.8 copy.55
  407.3 4.0 copy.56
  411.3 10.1 %fusion.12 = (f32[16,1536]{1,0:T(8,128)S(1)}, f32[16,128]{1,0:T(8,128)S(1)}, f32[16,128]{1,0:T(8,128)S(1)}, f32[16,1536]{1,0:T(8,128)S(1)}, f32[16,128,1536]{2,1,0:T(8,128)}) fusion(bf16[16,128,1536]{2,1,0:T(8,128)(2,1)} %param.7, f32[16,128]{1,0:T(8,128)S(1)} %add_rsqrt_fusion, f32[16,128]{1,0:T(8,128)S(1)} %broadcast_multiply_fusion.2, ...), kind=kOutput, calls=%fused_computation.16 | convolution fusion | flops 434057216 | bytes 19660800 | tf_op jit(solution)/shard_map/fto,od->ftd/dot_general | solution.py:50
  421.4 3.5 fusion.18
  424.9 0.7 pad_maximum_fusion
  425.7 66.1 %all-reduce.6.cloned.1.call-done = (f32[64,1536]{1,0:T(8,128)}, f32[16,2,1536]{2,0,1:T(8,128)}) async-done(((f32[64,1536]{1,0:T(8,128)}, f32[16,2,1536]{2,0,1:T(8,128)}), (f32[64,1536]{1,0:T(8,128)}, f32[16,2,1536]{2,0,1:T(8,128)})) %all-reduce.6.cloned.1.call-update) | async-done | bytes 589840 | tf_op jit(solution)/shard_map/psum | solution.py:53
  491.8 10.5 %fusion.11 = bf16[16,128,1536]{2,1,0:T(8,128)(2,1)} fusion(bf16[16,128,1536]{2,1,0:T(8,128)(2,1)} %param.7, f32[16,128,1536]{2,1,0:T(8,128)} %get-tuple-element.26, f32[16,128]{1,0:T(8,128)S(1)} %broadcast_multiply_fusion, f32[16,128]{1,0:T(8,128)S(1)} %broadcast_multiply_fusion.1, f32[16,1536]{1,0:T(8,128)S(1)} %get-tuple-element.28, ...), kind=kLoop, calls=%fused_computation.15 | loop fusion | flops 28311552 | bytes 25296896 | tf_op jit(solution)/shard_map/convert_element_type | solution.py:62
  502.3 0.8 copy.59
  503.2 135.7 %all-reduce.4.cloned.1.call-done = f32[64,1536]{1,0:T(8,128)} async-done(((f32[64,1536]{1,0:T(8,128)}), f32[64,1536]{1,0:T(8,128)}) %all-reduce.4.cloned.1.call-update) | async-done | bytes 393232 | tf_op jit(solution)/shard_map/psum | solution.py:54
  638.8 1.8 copy.81
  (40 shorter events, 0.8 us)
Async XLA Ops:
  7.2 8.7 %copy-start = (bf16[64,1536]{1,0:T(8,128)(2,1)S(1)}, bf16[64,1536]{1,0:T(8,128)(2,1)}, u32[]{:S(2)}) copy-start(bf16[64,1536]{1,0:T(8,128)(2,1)} %param.9) | copy-start | bytes 589828
  7.2 8.5 %copy-start.3 = (f32[16,2,1536]{2,1,0:T(2,128)S(1)}, f32[16,2,1536]{2,1,0:T(2,128)}, u32[]{:S(2)}) copy-start(f32[16,2,1536]{2,1,0:T(2,128)} %param.8) | copy-start | bytes 589828
  7.2 49.5 %all-gather.2.cloned.1.call-start = ((), (), s32[]{:S(2)}) async-start(), calls=%async_computation.3 | async-start | bytes 2359296 | tf_op jit(solution)/shard_map/all_gather | solution.py:29
  7.2 8.7 %copy-start.1 = (bf16[16,128,1536]{2,1,0:T(8,128)(2,1)S(1)}, bf16[16,128,1536]{2,1,0:T(8,128)(2,1)}, u32[]{:S(2)}) copy-start(bf16[16,128,1536]{2,1,0:T(8,128)(2,1)} %param.7) | copy-start | bytes 18874372
  72.0 30.4 %copy-start.5 = (s32[8]{0:T(128)S(1)}, s32[8]{0:T(128)}, u32[]{:S(2)}) copy-start(s32[8]{0:T(128)} %param.12) | copy-start | bytes 100
  92.8 58.5 %all-to-all-start = ((bf16[32,2,16384]{2,1,0:T(2,128)(2,1)}), bf16[32,2,16384]{2,1,0:T(2,128)(2,1)S(1)}, u32[]{:S(2)}, u32[]{:S(2)}) async-start(bf16[32,2,16384]{2,1,0:T(2,128)(2,1)} %reshape.132), calls=%async_computation | async-start | bytes 4194304 | tf_op jit(solution)/shard_map/all_to_all | solution.py:30
  102.4 301.0 %reduce-scatter.2.cloned.1.call-start = ((), (), s32[]{:S(2)}) async-start(), calls=%async_computation.4 | async-start | bytes 4718592 | tf_op jit(solution)/shard_map/reduce_scatter | solution.py:47
  165.7 16.0 %copy-start.2 = (bf16[8,21,16,128]{3,2,1,0:T(8,128)(2,1)S(1)}, bf16[8,21,16,128]{3,2,1,0:T(8,128)(2,1)}, u32[]{:S(2)}) copy-start(bf16[8,21,16,128]{3,2,1,0:T(8,128)(2,1)} %param.10) | copy-start | bytes 2064388
  165.7 77.7 %copy-start.6 = (s32[8]{0:T(128)S(1)}, s32[8]{0:T(128)}, u32[]{:S(2)}) copy-start(s32[8]{0:T(128)} %param.13) | copy-start | bytes 100
  352.7 139.1 %all-reduce.6.cloned.1.call-start = ((), (), s32[]{:S(2)}) async-start(), calls=%async_computation.6 | async-start | bytes 1179648 | tf_op jit(solution)/shard_map/psum | solution.py:53
  407.3 14.2 %slice-start = ((s8[6291456]{0:T(1024)(128)(4,1)}), s8[2097152]{0:T(1024)(128)(4,1)S(1)}, s32[]{:S(2)}) async-start(s8[6291456]{0:T(1024)(128)(4,1)} %bitcast.45), calls=%async_computation.7 | async-start | bytes 4194304
  411.3 10.1 %slice-start.1 = ((s8[6291456]{0:T(1024)(128)(4,1)}), s8[4194304]{0:T(1024)(128)(4,1)S(1)}, s32[]{:S(2)}) async-start(s8[6291456]{0:T(1024)(128)(4,1)} %bitcast.45), calls=%async_computation.8 | async-start | bytes 8388608
  425.6 213.2 %all-reduce.4.cloned.1.call-start = ((), (), s32[]{:S(2)}) async-start(), calls=%async_computation.5 | async-start | bytes 786432 | tf_op jit(solution)/shard_map/psum | solution.py:54
  491.8 10.5 %copy-start.4 = (f32[16,2,1536]{2,0,1:T(8,128)S(1)}, f32[16,2,1536]{2,0,1:T(8,128)}, u32[]{:S(2)}) copy-start(f32[16,2,1536]{2,0,1:T(8,128)} %get-tuple-element.23) | copy-start | bytes 589828
Sparse Core Ops, SparseCore 0:
  24.6 31.9 all-gather.1
  352.8 50.5 reduce-scatter.1
  425.7 66.0 all-reduce.5
  495.1 143.7 all-reduce.3
